TPU v7x, 32 devices: a whole 2x2x4 slice. The times are simulated.
32 devices in a mesh: grp: 4 (over z), fsdp: 8 (over y, x, core).
Axes of the slice: x: 2, y: 2, z: 4, core: 2. Of those that a mesh axis runs over, the one named last changes fastest.
Arguments:
- acts: bfloat16 [64, 128, 4096], P(('grp', 'fsdp'))
- out_grads: bfloat16 [64, 128, 1024], P(('grp', 'fsdp'))
- doc_lengths: int32 [64], P(('grp', 'fsdp')), may hold values from 32 to 128
- proj_in: bfloat16 [64, 4096], replicated, may hold values from -0.09375 to 0.09375
- proj_out: bfloat16 [64, 1024], replicated, may hold values from -0.1875 to 0.1875
- store_grads: bfloat16 [7168, 4096], P(('grp', 'fsdp')), may hold values from -6 to 6
- queries: bfloat16 [512, 4096], P('fsdp'), may hold values from -6 to 6
Outputs:
- new_grads: bfloat16 [64, 4096], P(('grp', 'fsdp'))
- store_scores: bfloat16 [7168, 512], P(('grp', 'fsdp'))
- new_scores: bfloat16 [64, 512], P(('grp', 'fsdp'))
All inputs are finite; a program needn't handle non-finite values.
Results may differ from a plain program's by a relative error of at most 0.012.
The roundings to bfloat16 on the way count: a program that leaves them out, or rounds other values in their place, can miss the bound.
Values may be sent and summed in bfloat16 or wider, within the bound.
A program may use at most 64 MiB of HBM per device.

v0:
```python
import jax
import jax.numpy as jnp
from jax import lax
from jax.sharding import PartitionSpec as P


def damped_inverse(summed, token_count, identity_matrix):
    proj_rank = identity_matrix.shape[0]
    covariance = summed / token_count
    damped = covariance + 0.1 * jnp.trace(covariance) / proj_rank * identity_matrix
    lower_factor = jnp.linalg.cholesky(damped)
    return jax.scipy.linalg.cho_solve((lower_factor, True), identity_matrix)


def precondition(query_rows, out_inverse, in_inverse):
    proj_rank = out_inverse.shape[0]
    query_mats = query_rows.astype(jnp.float32).reshape(query_rows.shape[0], proj_rank, proj_rank)
    half_done = jnp.einsum("ab,qbc->qac", out_inverse, query_mats, precision=lax.Precision.HIGHEST)
    precond = jnp.einsum("qac,cd->qad", half_done, in_inverse, precision=lax.Precision.HIGHEST)
    return precond.reshape(query_rows.shape[0], proj_rank * proj_rank).astype(jnp.bfloat16)


def project(tokens, projection):
    docs_here, length, features = tokens.shape
    flat = tokens.reshape(docs_here * length, features)
    result = lax.dot_general(
        flat, projection, (((1,), (1,)), ((), ())), preferred_element_type=jnp.float32
    )
    return result.reshape(docs_here, length, projection.shape[0])


def factor_totals(in_factor, out_factor, token_count):
    return lax.psum((in_factor, out_factor, token_count), ("grp", "fsdp"))


def shards(acts, out_grads, doc_lengths, proj_in, proj_out, store_grads, queries):
    docs_here, length, features = acts.shape
    proj_rank = proj_in.shape[0]
    identity_matrix = jnp.eye(proj_rank, dtype=jnp.float32)
    positions = lax.broadcasted_iota(jnp.int32, (docs_here, length), 1)
    valid_mask = (positions < doc_lengths[:, None]).astype(jnp.float32)
    in_proj = project(acts, proj_in)
    out_proj = project(out_grads, proj_out)
    in_masked = in_proj * valid_mask[:, :, None]
    out_masked = out_proj * valid_mask[:, :, None]
    in_factor = jnp.einsum("dta,dtb->ab", in_masked, in_proj, precision=lax.Precision.HIGHEST)
    out_factor = jnp.einsum("dta,dtb->ab", out_masked, out_proj, precision=lax.Precision.HIGHEST)
    token_count = jnp.sum(valid_mask)
    per_doc = jnp.einsum("dta,dtb->dab", out_masked, in_proj, precision=lax.Precision.HIGHEST)
    per_doc = per_doc / doc_lengths.astype(jnp.float32)[:, None, None]
    new_grads = per_doc.reshape(docs_here, proj_rank * proj_rank).astype(jnp.bfloat16)
    score_rows = jnp.concatenate([store_grads, new_grads], axis=0)
    stored = store_grads.shape[0]
    in_total, out_total, tokens_total = factor_totals(in_factor, out_factor, token_count)
    in_inverse = damped_inverse(in_total, tokens_total, identity_matrix)
    out_inverse = damped_inverse(out_total, tokens_total, identity_matrix)
    prepared_local = precondition(queries, out_inverse, in_inverse)
    scores = lax.dot_general(
        score_rows,
        lax.all_gather(prepared_local, "fsdp", axis=0, tiled=True),
        (((1,), (1,)), ((), ())),
        preferred_element_type=jnp.float32,
    )
    store_scores = scores[:stored].astype(jnp.bfloat16)
    new_scores = scores[stored:].astype(jnp.bfloat16)
    return (new_grads, store_scores, new_scores)


def solution(mesh):
    placed = (
        P(("grp", "fsdp"), None, None),
        P(("grp", "fsdp"), None, None),
        P(("grp", "fsdp")),
        P(),
        P(),
        P(("grp", "fsdp"), None),
        P("fsdp", None),
    )
    return jax.shard_map(
        shards,
        mesh=mesh,
        in_specs=placed,
        out_specs=(P(("grp", "fsdp"), None), P(("grp", "fsdp"), None), P(("grp", "fsdp"), None)),
        check_vma=False,
    )
```

profile of v0, /device:TPU:0, one launch (start us, length us, event | category | flops | bytes accessed | tf_op | source)
XLA Modules:
  0.0 139.9 jit_solution(4176288750345755124)
XLA Ops:
  7.2 0.0 copy-start
  7.2 0.0 copy-start.2
  7.2 0.0 copy-start.1
  7.2 0.0 all-gather.2.cloned.1.call-start
  7.2 1.5 %fusion.36 = f32[]{:T(128)} fusion(s32[2]{0:T(128)} %param.12), kind=kLoop, calls=%fused_computation.55 | loop fusion | flops 767 | bytes 12 | tf_op jit(solution)/shard_map/reduce_sum | solution.py:48
  8.7 0.7 compare_convert_fusion
  9.5 0.0 copy-done
  9.5 1.8 %fusion.13 = f32[2,128,64]{1,2,0:T(8,128)S(1)} fusion(bf16[2,128,4096]{2,1,0:T(8,128)(2,1)S(1)} %copy-done, bf16[64,4096]{1,0:T(8,128)(2,1)} %param.13), kind=kOutput, calls=%fused_computation.14 | convolution fusion | flops 134217728 | bytes 2686976 | tf_op jit(solution)/shard_map/dot_general | solution.py:26
  11.3 0.2 convolution_bitcast_fusion.1
  11.5 0.0 copy-done.2
  11.5 0.0 copy-done.1
  11.5 0.3 fusion.15
  11.8 0.2 convolution_bitcast_fusion.3
  12.0 42.9 %all-reduce = (f32[64,64]{0,1:T(8,128)S(1)}, f32[]{:T(128)}, f32[64,64]{0,1:T(8,128)S(1)}) all-reduce(f32[64,64]{0,1:T(8,128)S(1)} %convolution_bitcast_fusion.1, f32[]{:T(128)} %fusion.36, f32[64,64]{0,1:T(8,128)S(1)} %convolution_bitcast_fusion.3), channel_id=1, replica_groups=mesh['grp'=4,'fsdp'=8] {'grp','fsdp'}, use_global_device_ids=true, to_apply=%region_6.9 | all-reduce | flops 8193 | bytes 65544 | tf_op jit(solution)/shard_map/psum | solution.py:33
  54.9 1.3 select_reduce_fusion.3
  56.1 1.3 select_reduce_fusion.2
  58.7 0.7 select_add_fusion
  59.4 0.1 copy.13
  59.5 5.8 %cholesky.55 = f32[64,64]{1,0:T(8,128)S(1)} custom-call(f32[64,64]{1,0:T(8,128)S(1)} %fusion.28), custom_call_target="Cholesky" | custom-call | tf_op jit(solution)/shard_map/jit(cholesky)/cholesky | solution.py:11
  65.4 0.6 compare_reduce_fusion
  66.0 0.7 fusion.25
  66.7 4.9 %custom-call.9 = f32[1,64,64]{1,2,0:T(8,128)S(1)} custom-call(f32[1,64,64]{2,1,0:T(8,128)S(1)} %fusion.25), custom_call_target="InvertDiagBlocksLowerTriangular" | custom-call | tf_op jit(solution)/shard_map/jit(_cho_solve)/triangular_solve | solution.py:12
  71.6 0.3 fusion.20
  71.8 0.2 convolution_bitcast_fusion
  72.0 0.1 copy.11
  72.1 5.8 %cholesky.44 = f32[64,64]{1,0:T(8,128)S(1)} custom-call(f32[64,64]{1,0:T(8,128)S(1)} %fusion.31), custom_call_target="Cholesky" | custom-call | tf_op jit(solution)/shard_map/jit(cholesky)/cholesky | solution.py:11
  78.0 0.6 compare_reduce_fusion.1
  78.6 0.7 fusion.24
  79.3 4.9 %custom-call.8 = f32[1,64,64]{1,2,0:T(8,128)S(1)} custom-call(f32[1,64,64]{2,1,0:T(8,128)S(1)} %fusion.24), custom_call_target="InvertDiagBlocksLowerTriangular" | custom-call | tf_op jit(solution)/shard_map/jit(_cho_solve)/triangular_solve | solution.py:12
  84.2 0.3 fusion.22
  84.4 0.2 convolution_bitcast_fusion.2
  84.6 2.1 %reshape.52 = bf16[64,64,64]{2,1,0:T(8,128)(2,1)S(1)} reshape(bf16[64,4096]{1,0:T(8,128)(2,1)} %param.16) | data formatting | bytes 1048576 | tf_op jit(solution)/shard_map/reshape | solution.py:17
  86.7 1.0 fusion.37
  87.6 0.0 copy-start.4
  87.7 1.8 %fusion.6 = bf16[64,64,64]{2,1,0:T(8,128)(2,1)S(1)} fusion(f32[64,64,1]{1,0,2:T(8,128)S(1)} %convolution_bitcast_fusion, f32[64,64,64]{2,0,1:T(8,128)S(1)} %fusion.37), kind=kOutput, calls=%fused_computation.6 | convolution fusion | flops 201588736 | bytes 1589248 | tf_op jit(solution)/shard_map/qac,cd->qad/dot_general | solution.py:19
  89.4 1.6 %convert_element_type.36 = bf16[64,4096]{1,0:T(8,128)(2,1)} reshape(bf16[64,64,64]{2,1,0:T(8,128)(2,1)S(1)} %fusion.6) | data formatting | bytes 1048576 | tf_op jit(solution)/shard_map/convert_element_type | solution.py:20
  91.1 0.0 all-gather.2.cloned.1.call-update
  91.1 0.0 copy-done.4
  91.1 0.2 fusion.12
  91.3 0.1 convert_element_type.33
  91.4 0.0 copy-start.3
  91.5 36.3 %all-gather.2.cloned.1.call-done = bf16[512,4096]{1,0:T(8,128)(2,1)} async-done(((bf16[64,4096]{1,0:T(8,128)(2,1)}), bf16[512,4096]{1,0:T(8,128)(2,1)}) %all-gather.2.cloned.1.call-update) | async-done | bytes 4194320 | tf_op jit(solution)/shard_map/all_gather | solution.py:60
  127.8 4.0 %fusion.9 = bf16[226,512]{1,0:T(8,128)(2,1)S(1)} fusion(bf16[512,4096]{1,0:T(8,128)(2,1)} %all-gather.2.cloned.1.call-done, bf16[2,4096]{1,0:T(2,128)(2,1)S(1)} %convert_element_type.33, bf16[224,4096]{1,0:T(8,128)(2,1)} %param.15), kind=kOutput, calls=%fused_computation.7 | convolution fusion | flops 951731200 | bytes 6277120 | tf_op jit(solution)/shard_map/dot_general | solution.py:58
  131.8 0.0 copy-done.3
  131.8 0.6 slice.23
  132.4 0.7 slice.22
  (5 shorter events, 0.1 us)
Async XLA Ops:
  7.2 2.3 %copy-start = (bf16[2,128,4096]{2,1,0:T(8,128)(2,1)S(1)}, bf16[2,128,4096]{2,1,0:T(8,128)(2,1)}, u32[]{:S(2)}) copy-start(bf16[2,128,4096]{2,1,0:T(8,128)(2,1)} %param.10) | copy-start | bytes 6291460
  7.2 4.3 %copy-start.2 = (bf16[64,1024]{1,0:T(8,128)(2,1)S(1)}, bf16[64,1024]{1,0:T(8,128)(2,1)}, u32[]{:S(2)}) copy-start(bf16[64,1024]{1,0:T(8,128)(2,1)} %param.14) | copy-start | bytes 393220
  7.2 4.3 %copy-start.1 = (bf16[2,128,1024]{2,1,0:T(8,128)(2,1)S(1)}, bf16[2,128,1024]{2,1,0:T(8,128)(2,1)}, u32[]{:S(2)}) copy-start(bf16[2,128,1024]{2,1,0:T(8,128)(2,1)} %param.11) | copy-start | bytes 1572868
  7.2 120.6 %all-gather.2.cloned.1.call-start = ((), (), s32[]{:S(2)}) async-start(), calls=%async_computation | async-start | bytes 4718592 | tf_op jit(solution)/shard_map/all_gather | solution.py:60
  87.6 3.4 %copy-start.4 = (s32[2]{0:T(128)S(1)}, s32[2]{0:T(128)}, u32[]{:S(2)}) copy-start(s32[2]{0:T(128)} %param.12) | copy-start | bytes 28
  91.4 40.4 %copy-start.3 = (bf16[2,4096]{1,0:T(2,128)(2,1)}, bf16[2,4096]{1,0:T(2,128)(2,1)S(1)}, u32[]{:S(2)}) copy-start(bf16[2,4096]{1,0:T(2,128)(2,1)S(1)} %convert_element_type.33) | copy-start | bytes 49156
Sparse Core Ops, SparseCore 0:
  91.2 36.5 all-gather.1
where the time goes:
time: 140 us
  blocking collectives  42.9 us (31%)
  waiting for transfers between devices  36.3 us (26%)
  other arithmetic  29.5 us (21%)
  between operations  15.6 us (11%)
  matrix products  10.3 us (7%)
  local copies, waits for them, and re-layouts  5.25 us (4%)
    psum x1, blocking collectives, factor_totals(): return lax.psum((in_factor, out_factor, token_count), ('grp', 'fsdp'))  42.9 us
    all_gather x1, waiting for transfers between devices, shards(): lax.all_gather(prepared_local, 'fsdp', axis=0, tiled=True)  36.3 us
    another operation x6, other arithmetic, damped_inverse(): lower_factor = jnp.linalg.cholesky(damped)  13 us
    another operation x4, other arithmetic, damped_inverse(): return jax.scipy.linalg.cho_solve((lower_factor, True), identity_matrix)  11.1 us
    dot_general x1, matrix products, shards(): lax.dot_general(score_rows, lax.all_gather(prepared_local, 'fsdp', axis=0...  4.03 us
  transfers between devices with their start and end apart: 1, of which 1 were waited for; matrix products, arithmetic and copies ran while one was open for 0% of the time, Pallas kernels for 0%

commit v1 on v0

--- a/solution.py
+++ b/solution.py
@@ -2,6 +2,28 @@
 import jax.numpy as jnp
 from jax import lax
 from jax.sharding import PartitionSpec as P
+
+
+def laid_out(blocks, dim):
+    blocks = jnp.moveaxis(blocks, 0, dim)
+    shape = blocks.shape
+    return blocks.reshape(*shape[:dim], shape[dim] * shape[dim + 1], *shape[dim + 2 :])
+
+
+def doubled(shard, axis):
+    devices = lax.axis_size(axis)
+    pieces = shard[None]
+    for level in range(devices.bit_length() - 1):
+        bit = 1 << level
+        theirs = lax.ppermute(pieces, axis, [(i, i ^ bit) for i in range(devices)])
+        both = jnp.stack([pieces, theirs])
+        upper = lax.axis_index(axis) >> level & 1
+        pieces = jnp.where(upper == 0, both, both[::-1]).reshape(-1, *shard.shape)
+    return pieces
+
+
+def doubled_up(array, axis, dim):
+    return laid_out(doubled(array, axis), dim)
 
 
 def damped_inverse(summed, token_count, identity_matrix):
@@ -57,7 +79,7 @@
     prepared_local = precondition(queries, out_inverse, in_inverse)
     scores = lax.dot_general(
         score_rows,
-        lax.all_gather(prepared_local, "fsdp", axis=0, tiled=True),
+        doubled_up(prepared_local, "fsdp", 0),
         (((1,), (1,)), ((), ())),
         preferred_element_type=jnp.float32,
     )

time: 140 us -> 173 us (1.24)
  waiting for transfers between devices: 36.3 us -> 69.8 us
  between operations: 15.6 us -> 2.18 us
  other arithmetic: 29.5 us -> 39.1 us
  starting transfers between devices: 0.04 us -> 4.01 us
  matrix products: 10.3 us -> 7.61 us
  local copies, waits for them, and re-layouts: 5.25 us -> 7.38 us
    ppermute x0 -> x3, waiting for transfers between devices: none -> 69.8 us  [doubled(): theirs = lax.ppermute(pieces, axis, [(i, i ^ bit) for i in range(devices)])]
    all_gather x1 -> x0, waiting for transfers between devices: 36.3 us -> none  [shards(): lax.all_gather(prepared_local, 'fsdp', axis=0, tiled=True)]
    another operation x0 -> x4, other arithmetic: none -> 6.61 us  [doubled(): both = jnp.stack([pieces, theirs])]
    ppermute x0 -> x3, starting transfers between devices: none -> 4.01 us  [doubled(): theirs = lax.ppermute(pieces, axis, [(i, i ^ bit) for i in range(devices)])]
    select_n x0 -> x2, other arithmetic: none -> 2.96 us  [doubled(): pieces = jnp.where(upper == 0, both, both[::-1]).reshape(-1, *shard.shape)]
    dot_general x1, matrix products: 4.03 us -> 1.29 us  [shards(): lax.dot_general(score_rows, doubled_up(prepared_local, 'fsdp', 0), (((1,)...]
  transfers between devices with their start and end apart: 1 -> 3, of which waited for: 1 -> 3; matrix products, arithmetic and copies ran while one was open for 0% -> 1% of each run, Pallas kernels for 0% -> 0%
where the time goes in v1:
time: 173 us
  waiting for transfers between devices  69.8 us (40%)
  blocking collectives  42.9 us (25%)
  other arithmetic  39.1 us (23%)
  matrix products  7.61 us (4%)
  local copies, waits for them, and re-layouts  7.38 us (4%)
  starting transfers between devices  4.01 us (2%)
  between operations  2.18 us (1%)
    ppermute x3, waiting for transfers between devices, doubled(): theirs = lax.ppermute(pieces, axis, [(i, i ^ bit) for i in range(devices)])  69.8 us
    psum x1, blocking collectives, factor_totals(): return lax.psum((in_factor, out_factor, token_count), ('grp', 'fsdp'))  42.9 us
    another operation x6, other arithmetic, damped_inverse(): lower_factor = jnp.linalg.cholesky(damped)  13 us
    another operation x4, other arithmetic, damped_inverse(): return jax.scipy.linalg.cho_solve((lower_factor, True), identity_matrix)  11.1 us
    another operation x4, other arithmetic, doubled(): both = jnp.stack([pieces, theirs])  6.61 us
    ppermute x3, starting transfers between devices, doubled(): theirs = lax.ppermute(pieces, axis, [(i, i ^ bit) for i in range(devices)])  4.01 us
  transfers between devices with their start and end apart: 3, of which 3 were waited for; matrix products, arithmetic and copies ran while one was open for 1% of the time, Pallas kernels for 0%

profile of v1, /device:TPU:0, one launch (start us, length us, event | category | flops | bytes accessed | tf_op | source)
XLA Modules:
  0.0 172.9 jit_solution(6468890517854114027)
XLA Ops:
  0.6 0.0 copy-start
  0.7 1.5 fusion.38
  2.1 0.7 compare_convert_fusion
  2.9 1.8 %fusion.15 = f32[2,128,64]{1,2,0:T(8,128)S(1)} fusion(bf16[2,128,4096]{2,1,0:T(8,128)(2,1)S(1)} %copy-done, bf16[64,4096]{1,0:T(8,128)(2,1)} %param.13), kind=kOutput, calls=%fused_computation.22 | convolution fusion | flops 134217728 | bytes 2686976 | tf_op jit(solution)/shard_map/dot_general | solution.py:48
  4.7 0.2 convolution_bitcast_fusion.1
  4.9 0.3 fusion.17
  5.2 0.2 convolution_bitcast_fusion.3
  5.4 42.9 %all-reduce = (f32[64,64]{0,1:T(8,128)S(1)}, f32[]{:T(128)}, f32[64,64]{0,1:T(8,128)S(1)}) all-reduce(f32[64,64]{0,1:T(8,128)S(1)} %convolution_bitcast_fusion.1, f32[]{:T(128)} %fusion.38, f32[64,64]{0,1:T(8,128)S(1)} %convolution_bitcast_fusion.3), channel_id=1, replica_groups=mesh['grp'=4,'fsdp'=8] {'grp','fsdp'}, use_global_device_ids=true, to_apply=%region_6.9 | all-reduce | flops 8193 | bytes 65544 | tf_op jit(solution)/shard_map/psum | solution.py:55
  48.3 1.3 select_reduce_fusion.3
  49.6 1.3 select_reduce_fusion.2
  52.1 0.7 select_add_fusion
  52.8 0.1 copy.13
  52.9 5.8 %cholesky.55 = f32[64,64]{1,0:T(8,128)S(1)} custom-call(f32[64,64]{1,0:T(8,128)S(1)} %fusion.30), custom_call_target="Cholesky" | custom-call | tf_op jit(solution)/shard_map/jit(cholesky)/cholesky | solution.py:33
  58.8 0.6 compare_reduce_fusion
  59.4 0.7 fusion.27
  60.1 4.9 %custom-call.9 = f32[1,64,64]{1,2,0:T(8,128)S(1)} custom-call(f32[1,64,64]{2,1,0:T(8,128)S(1)} %fusion.27), custom_call_target="InvertDiagBlocksLowerTriangular" | custom-call | tf_op jit(solution)/shard_map/jit(_cho_solve)/triangular_solve | solution.py:34
  65.0 0.3 fusion.22
  65.2 0.2 convolution_bitcast_fusion
  65.4 0.1 copy.11
  65.5 5.8 %cholesky.44 = f32[64,64]{1,0:T(8,128)S(1)} custom-call(f32[64,64]{1,0:T(8,128)S(1)} %fusion.33), custom_call_target="Cholesky" | custom-call | tf_op jit(solution)/shard_map/jit(cholesky)/cholesky | solution.py:33
  71.4 0.6 compare_reduce_fusion.1
  72.0 0.7 fusion.26
  72.7 4.9 %custom-call.8 = f32[1,64,64]{1,2,0:T(8,128)S(1)} custom-call(f32[1,64,64]{2,1,0:T(8,128)S(1)} %fusion.26), custom_call_target="InvertDiagBlocksLowerTriangular" | custom-call | tf_op jit(solution)/shard_map/jit(_cho_solve)/triangular_solve | solution.py:34
  77.6 0.3 fusion.24
  77.8 0.2 convolution_bitcast_fusion.2
  78.0 2.2 %reshape.79 = bf16[64,64,64]{2,1,0:T(8,128)(2,1)S(1)} reshape(bf16[64,4096]{1,0:T(8,128)(2,1)} %param.16) | data formatting | bytes 1048576 | tf_op jit(solution)/shard_map/reshape | solution.py:39
  80.2 1.0 fusion.39
  81.2 1.8 %fusion.6 = bf16[64,64,64]{2,1,0:T(8,128)(2,1)S(1)} fusion(f32[64,64,1]{1,0,2:T(8,128)S(1)} %convolution_bitcast_fusion, f32[64,64,64]{2,0,1:T(8,128)S(1)} %fusion.39), kind=kOutput, calls=%fused_computation.11 | convolution fusion | flops 201588736 | bytes 1589248 | tf_op jit(solution)/shard_map/qac,cd->qad/dot_general | solution.py:41
  83.0 1.6 convert_element_type.54
  84.6 1.6 convert_element_type.53
  86.3 0.6 collective-permute-done
  86.9 1.3 pad_maximum_fusion.2
  88.2 1.3 fusion.14
  89.5 2.3 %collective-permute-start.1 = (bf16[2,64,4096]{2,1,0:T(8,128)(2,1)}, bf16[2,64,4096]{2,1,0:T(8,128)(2,1)}, u32[]{:S(2)}, u32[]{:S(2)}) collective-permute-start(bf16[2,64,4096]{2,1,0:T(8,128)(2,1)} %get-tuple-element.9), channel_id=1, source_target_pairs={{0,2},{1,3},{2,0},{3,1},{4,6},{5,7},{6,4},{7,5},{8,10},{9,11},{10,... | collective-permute-start | bytes 3145736 | tf_op jit(solution)/shard_map/ppermute | solution.py:18
  91.7 23.8 %collective-permute-done.1 = bf16[2,64,4096]{2,1,0:T(8,128)(2,1)} collective-permute-done((bf16[2,64,4096]{2,1,0:T(8,128)(2,1)}, bf16[2,64,4096]{2,1,0:T(8,128)(2,1)}, u32[]{:S(2)}, u32[]{:S(2)}) %collective-permute-start.1) | collective-permute-done | bytes 1048608 | tf_op jit(solution)/shard_map/ppermute | solution.py:18
  115.5 1.4 pad_maximum_fusion.1
  116.9 0.0 copy-start.5
  116.9 1.8 %reverse_select_fusion.1 = bf16[2,2,64,4096]{3,2,1,0:T(8,128)(2,1)} fusion(bf16[2,2,64,4096]{3,2,1,0:T(8,128)(2,1)S(1)} %pad_maximum_fusion.1, pred[]{:T(512)S(6)} %eq.26), kind=kLoop, calls=%fused_computation.2 | loop fusion | flops 1048576 | bytes 4194305 | tf_op jit(solution)/shard_map/jit(_where)/select_n | solution.py:21
  118.8 1.7 %collective-permute-start.2 = (bf16[4,64,4096]{2,1,0:T(8,128)(2,1)}, bf16[4,64,4096]{2,1,0:T(8,128)(2,1)}, u32[]{:S(2)}, u32[]{:S(2)}) collective-permute-start(bf16[4,64,4096]{2,1,0:T(8,128)(2,1)} %bitcast.18), channel_id=1, source_target_pairs={{0,4},{1,5},{2,6},{3,7},{4,0},{5,1},{6,2},{7,3},{8,12},{9,13},{10,... | collective-permute-start | bytes 6291464 | tf_op jit(solution)/shard_map/ppermute | solution.py:18
  120.5 0.2 fusion.12
  120.8 0.1 convert_element_type.50
  120.9 45.4 %collective-permute-done.2 = bf16[4,64,4096]{2,1,0:T(8,128)(2,1)} collective-permute-done((bf16[4,64,4096]{2,1,0:T(8,128)(2,1)}, bf16[4,64,4096]{2,1,0:T(8,128)(2,1)}, u32[]{:S(2)}, u32[]{:S(2)}) %collective-permute-start.2) | collective-permute-done | bytes 2097184 | tf_op jit(solution)/shard_map/ppermute | solution.py:18
  166.2 2.6 %pad_maximum_fusion = bf16[2,4,64,4096]{3,2,1,0:T(8,128)(2,1)S(1)} fusion(bf16[1,4,64,4096]{3,2,1,0:T(8,128)(2,1)} %bitcast.19, bf16[1,4,64,4096]{3,2,1,0:T(8,128)(2,1)} %bitcast.17), kind=kLoop, calls=%fused_computation.1 | loop fusion | flops 2097152 | bytes 8388608 | tf_op jit(solution)/shard_map/stack | solution.py:19
  168.9 1.1 reverse_select_fusion
  170.0 0.3 copy-done.4
  170.4 1.3 fusion.9
  171.6 0.6 slice.23
  172.2 0.7 slice.22
  (15 shorter events, 0.1 us)
Async XLA Ops:
  0.6 2.2 %copy-start = (bf16[2,128,4096]{2,1,0:T(8,128)(2,1)S(1)}, bf16[2,128,4096]{2,1,0:T(8,128)(2,1)}, u32[]{:S(2)}) copy-start(bf16[2,128,4096]{2,1,0:T(8,128)(2,1)} %param.10) | copy-start | bytes 6291460
  0.6 4.2 %copy-start.2 = (bf16[64,1024]{1,0:T(8,128)(2,1)S(1)}, bf16[64,1024]{1,0:T(8,128)(2,1)}, u32[]{:S(2)}) copy-start(bf16[64,1024]{1,0:T(8,128)(2,1)} %param.14) | copy-start | bytes 393220
  0.7 4.2 %copy-start.1 = (bf16[2,128,1024]{2,1,0:T(8,128)(2,1)S(1)}, bf16[2,128,1024]{2,1,0:T(8,128)(2,1)}, u32[]{:S(2)}) copy-start(bf16[2,128,1024]{2,1,0:T(8,128)(2,1)} %param.11) | copy-start | bytes 1572868
  84.6 2.3 %collective-permute-start = (bf16[1,64,4096]{2,1,0:T(8,128)(2,1)}, bf16[1,64,4096]{2,1,0:T(8,128)(2,1)}, u32[]{:S(2)}, u32[]{:S(2)}) collective-permute-start(bf16[1,64,4096]{2,1,0:T(8,128)(2,1)} %convert_element_type.54), channel_id=1, source_target_pairs={{0,1},{1,0},{2,3},{3,2},{4,5},{5,4},{6,7},{7,6},{8,9},{9,8},{10,11... | collective-permute-start | bytes 1572872 | tf_op jit(solution)/shard_map/ppermute | solution.py:18
  89.5 26.0 %collective-permute-start.1 = (bf16[2,64,4096]{2,1,0:T(8,128)(2,1)}, bf16[2,64,4096]{2,1,0:T(8,128)(2,1)}, u32[]{:S(2)}, u32[]{:S(2)}) collective-permute-start(bf16[2,64,4096]{2,1,0:T(8,128)(2,1)} %get-tuple-element.9), channel_id=1, source_target_pairs={{0,2},{1,3},{2,0},{3,1},{4,6},{5,7},{6,4},{7,5},{8,10},{9,11},{10,... | collective-permute-start | bytes 3145736 | tf_op jit(solution)/shard_map/ppermute | solution.py:18
  116.9 3.6 %copy-start.5 = (s32[2]{0:T(128)S(1)}, s32[2]{0:T(128)}, u32[]{:S(2)}) copy-start(s32[2]{0:T(128)} %param.12) | copy-start | bytes 28
  118.8 47.5 %collective-permute-start.2 = (bf16[4,64,4096]{2,1,0:T(8,128)(2,1)}, bf16[4,64,4096]{2,1,0:T(8,128)(2,1)}, u32[]{:S(2)}, u32[]{:S(2)}) collective-permute-start(bf16[4,64,4096]{2,1,0:T(8,128)(2,1)} %bitcast.18), channel_id=1, source_target_pairs={{0,4},{1,5},{2,6},{3,7},{4,0},{5,1},{6,2},{7,3},{8,12},{9,13},{10,... | collective-permute-start | bytes 6291464 | tf_op jit(solution)/shard_map/ppermute | solution.py:18
  120.9 49.2 %copy-start.3 = (bf16[2,4096]{1,0:T(2,128)(2,1)}, bf16[2,4096]{1,0:T(2,128)(2,1)S(1)}, u32[]{:S(2)}) copy-start(bf16[2,4096]{1,0:T(2,128)(2,1)S(1)} %convert_element_type.50) | copy-start | bytes 49156
  168.8 1.5 copy-start.4
